TPU v7x, 256 devices: a whole 4x4x8 slice. The times are simulated.
256 devices in a mesh: section: 32 (over x_lo, z, core), expert: 8 (over x_hi, y).
Axes of the slice: x: 4 (x_hi: 2, x_lo: 2; x = x_hi * 2 + x_lo), y: 4, z: 8, core: 2. Of those that a mesh axis runs over, the one named last changes fastest.
Arguments:
- tokens: bfloat16 [2048, 3072], P(('section', 'expert')), may hold values from -6 to 6
- upstream: bfloat16 [2048, 3072], P(('section', 'expert')), may hold values from -2 to 2
- route_ids: int32 [2048, 2], P(('section', 'expert')), may hold values from 0 to 7, all different within a row; in each aligned block of 8 rows (0 to 7, 8 to 15, ...) at most 4 rows name the same one
- route_gates: bfloat16 [2048, 2], P(('section', 'expert')), may hold values from 0.099609375 to 0.8984375
- w_gate: bfloat16 [8, 3072, 8192], P('expert', None, 'section'), may hold values from -0.109375 to 0.109375
- w_up: bfloat16 [8, 3072, 8192], P('expert', None, 'section'), may hold values from -0.109375 to 0.109375
- w_down: bfloat16 [8, 8192, 3072], P('expert', 'section'), may hold values from -0.0625 to 0.0625
Outputs:
- grad_tokens: bfloat16 [2048, 3072], P(('section', 'expert'))
- grad_gates: float32 [2048, 2], P(('section', 'expert'))
- grad_w_gate: bfloat16 [8, 3072, 8192], P('expert', None, 'section')
- grad_w_up: bfloat16 [8, 3072, 8192], P('expert', None, 'section')
- grad_w_down: bfloat16 [8, 8192, 3072], P('expert', 'section')
Inputs may be any that keep to these rules, and one draw needn't show every extreme that they name: `route_ids`: the two experts of a token differ. Among the 16 choices of the tokens of one device, each expert is named at most 4 times, and in some device's tokens some expert is named exactly 4 times.
All inputs are finite; a program needn't handle non-finite values.
Results may differ from a plain program's by a relative error of at most 0.0058.
Values may be sent and summed in bfloat16 or wider, within the bound.
A program may use at most 128 MiB of HBM per device.

v0:
```python
import jax
import jax.numpy as jnp
from jax import lax
from jax.sharding import PartitionSpec as P


def slot_matrix(route_ids, experts, capacity):
    flattened = route_ids.reshape(-1)
    onehot = (flattened[:, None] == jnp.arange(experts, dtype=jnp.int32)[None, :]).astype(jnp.int32)
    before = jnp.cumsum(onehot, axis=0) - onehot
    position = jnp.sum(before * onehot, axis=1)
    target = flattened * capacity + position
    columns = jnp.arange(experts * capacity, dtype=jnp.int32)
    return target[:, None] == columns[None, :]


def contract_last(left, right):
    return lax.dot_general(
        left, right, (((1,), (1,)), ((), ())), preferred_element_type=jnp.float32
    )


def contract_first(left, right):
    return lax.dot_general(
        left, right, (((0,), (0,)), ((), ())), preferred_element_type=jnp.float32
    )


def local(tokens, upstream, route_ids, route_gates, w_gate, w_up, w_down):
    experts = lax.axis_size("expert")
    tok_count, features = tokens.shape
    capacity = min(tok_count, max(2, 4 * tok_count // experts))
    chosen_slots = slot_matrix(route_ids, experts, capacity)
    placement = chosen_slots.astype(jnp.bfloat16)
    gates = route_gates.reshape(-1).astype(jnp.float32)
    tokens_twice = jnp.repeat(tokens, 2, axis=0)
    scaled = (gates[:, None] * jnp.repeat(upstream, 2, axis=0).astype(jnp.float32)).astype(
        jnp.bfloat16
    )
    send_x = contract_first(placement, tokens_twice).astype(jnp.bfloat16)
    send_u = contract_first(placement, scaled).astype(jnp.bfloat16)
    send = jnp.concatenate(
        [send_x.reshape(experts, capacity, features), send_u.reshape(experts, capacity, features)],
        axis=1,
    )
    recv = lax.all_to_all(send, "expert", split_axis=0, concat_axis=0, tiled=True)
    mine = jnp.stack([recv[:, :capacity], recv[:, capacity:]]).reshape(
        2, experts * capacity, features
    )
    every = lax.all_gather(mine, "section", axis=1, tiled=True)
    rows_x, rows_u = (every[0], every[1])
    gate_slab = w_gate[0]
    up_slab = w_up[0]
    down_slab = w_down[0]
    pre_gate = jnp.dot(rows_x, gate_slab, preferred_element_type=jnp.float32)
    pre_up = jnp.dot(rows_x, up_slab, preferred_element_type=jnp.float32)
    sigmoid_gate = jax.nn.sigmoid(pre_gate)
    active = pre_gate * sigmoid_gate
    hidden = (active * pre_up).astype(jnp.bfloat16)
    d_hidden = contract_last(rows_u, down_slab)
    d_gate = (d_hidden * pre_up * (sigmoid_gate * (1.0 + pre_gate * (1.0 - sigmoid_gate)))).astype(
        jnp.bfloat16
    )
    d_up = (d_hidden * active).astype(jnp.bfloat16)
    grad_down = contract_first(hidden, rows_u)
    grad_gate = contract_first(rows_x, d_gate)
    grad_up = contract_first(rows_x, d_up)
    input_part = contract_last(d_gate, gate_slab) + contract_last(d_up, up_slab)
    gate_part = hidden.astype(jnp.float32) * d_hidden
    units = gate_part.shape[1]
    gate_part = sum((gate_part[:, i : i + 128] for i in range(0, units, 128)))
    part = jnp.concatenate([input_part, gate_part], axis=1)
    part_mine = lax.psum_scatter(part, "section", scatter_dimension=0, tiled=True)
    back = lax.all_to_all(
        part_mine.reshape(experts, capacity, features + 128),
        "expert",
        split_axis=0,
        concat_axis=0,
        tiled=True,
    ).reshape(experts * capacity, features + 128)
    selector = chosen_slots.astype(jnp.float32)
    choice = jnp.dot(selector, back, precision=lax.Precision.HIGHEST)
    grad_tokens = jnp.sum(choice[:, :features].reshape(tok_count, 2, features), axis=1)
    grad_gates = (jnp.sum(choice[:, features:], axis=1) / gates).reshape(tok_count, 2)
    return (
        grad_tokens.astype(jnp.bfloat16),
        grad_gates,
        grad_gate.astype(jnp.bfloat16)[None],
        grad_up.astype(jnp.bfloat16)[None],
        grad_down.astype(jnp.bfloat16)[None],
    )


def solution(mesh):
    placed = (
        P(("section", "expert"), None),
        P(("section", "expert"), None),
        P(("section", "expert"), None),
        P(("section", "expert"), None),
        P("expert", None, "section"),
        P("expert", None, "section"),
        P("expert", "section", None),
    )
    return jax.shard_map(
        local,
        mesh=mesh,
        in_specs=placed,
        out_specs=(
            P(("section", "expert"), None),
            P(("section", "expert"), None),
            P("expert", None, "section"),
            P("expert", None, "section"),
            P("expert", "section", None),
        ),
        check_vma=False,
    )
```

profile of v0, /device:TPU:2, one launch (start us, length us, event | category | flops | bytes accessed | tf_op | source)
XLA Modules:
  0.0 304.9 jit_solution(16035402707329511470)
XLA Ops:
  7.2 0.0 copy-start
  7.2 0.0 all-gather.2.cloned.1.call-start
  7.2 0.9 copy.17
  8.1 0.1 reshape.64
  8.2 0.8 copy.16
  8.9 0.1 reshape.57
  9.0 0.1 fusion.21
  9.1 0.2 select_reduce_fusion
  9.3 0.9 broadcast_in_dim.19
  10.2 0.3 convolution_convert_fusion.1
  10.5 0.1 reshape.59
  10.6 0.9 broadcast_in_dim.20
  11.5 0.1 convert_element_type.63
  11.6 0.3 convolution_convert_fusion
  11.9 0.1 reshape.60
  12.0 0.2 pad_maximum_fusion.1
  12.2 16.0 %all_to_all.10 = bf16[8,8,3072]{2,1,0:T(8,128)(2,1)S(1)} all-to-all(bf16[8,8,3072]{2,1,0:T(8,128)(2,1)S(1)} %pad_maximum_fusion.1), channel_id=1, replica_groups=mesh['section'=32,'expert'=8] {'expert'}, dimensions={0} | all-to-all | bytes 786432 | tf_op jit(solution)/shard_map/all_to_all | solution.py:46
  28.3 0.1 fusion.25
  28.5 0.8 pad_maximum_fusion.2
  29.3 0.0 all-gather.2.cloned.1.call-update
  29.3 0.0 copy-start.2
  29.3 0.0 reduce-scatter.2.cloned.1.call-start
  29.4 79.5 %all-gather.2.cloned.1.call-done = bf16[2,1024,3072]{2,1,0:T(8,128)(2,1)} async-done(((bf16[2,32,3072]{2,1,0:T(8,128)(2,1)}), bf16[2,1024,3072]{2,1,0:T(8,128)(2,1)}) %all-gather.2.cloned.1.call-update) | async-done | bytes 12582928 | tf_op jit(solution)/shard_map/all_gather | solution.py:50
  108.8 4.8 %fusion.4 = f32[1024,256]{0,1:T(8,128)S(1)} fusion(bf16[2,1024,3072]{2,1,0:T(8,128)(2,1)} %all-gather.2.cloned.1.call-done, bf16[1,3072,256]{2,1,0:T(8,128)(2,1)S(1)} %copy-done), kind=kOutput, calls=%fused_computation.8 | convolution fusion | flops 1610612736 | bytes 8912896 | tf_op jit(solution)/shard_map/dot_general | solution.py:55
  113.6 1.6 copy-done.5
  115.2 1.9 fusion.5
  117.1 3.2 %convert_multiply_fusion = (f32[1024,256]{0,1:T(8,128)S(1)}, bf16[1024,256]{0,1:T(8,128)(2,1)}, bf16[1024,256]{0,1:T(8,128)(2,1)}, bf16[1024,256]{0,1:T(8,128)(2,1)S(1)}) fusion(f32[1024,256]{0,1:T(8,128)S(1)} %fusion.5, f32[1024,256]{0,1:T(8,128)S(1)} %fusion.4, bf16[1,256,3072]{2,1,0:T(8,128)(2,1)S(1)} %copy-done.6, bf16[2,1024,3072]{2,1,0:T(8,128)(2,1)S(1)} %copy-done.5), kind=kOutput, calls=%fused_computation.24 | convolution fusion | flops 1615069184 | bytes 12582912 | tf_op jit(solution)/shard_map/dot_general | solution.py:18
  120.3 0.1 slice_add_fusion
  120.3 0.2 copy.18
  120.6 3.0 fusion.12
  123.6 6.5 %convolution_add_fusion = f32[1024,3072]{1,0:T(8,128)} fusion(f32[1024,3072]{1,0:T(8,128)S(1)} %fusion.12, bf16[1024,256]{0,1:T(8,128)(2,1)S(1)} %get-tuple-element.18, bf16[1,3072,256]{2,1,0:T(8,128)(2,1)S(1)} %copy-done.3), kind=kOutput, calls=%fused_computation.1 | convolution fusion | flops 1613758464 | bytes 27262976 | tf_op jit(solution)/shard_map/dot_general | solution.py:18
  130.1 10.3 %pad_maximum_fusion = f32[1024,3200]{1,0:T(8,128)} fusion(f32[1024,128]{1,0:T(8,128)S(1)} %copy.18, f32[1024,3072]{1,0:T(8,128)} %convolution_add_fusion), kind=kLoop, calls=%fused_computation | loop fusion | flops 3276800 | bytes 26214400 | tf_op jit(solution)/shard_map/concatenate | solution.py:72
  140.4 0.0 reduce-scatter.2.cloned.1.call-update
  140.4 1.0 copy-done.4
  141.4 6.0 %fusion.11 = bf16[1,3072,256]{2,1,0:T(8,128)(2,1)} fusion(bf16[1024,256]{0,1:T(8,128)(2,1)S(1)} %copy-done.4, bf16[2,1024,3072]{2,1,0:T(8,128)(2,1)} %all-gather.2.cloned.1.call-done), kind=kOutput, calls=%fused_computation.15 | convolution fusion | flops 1611399168 | bytes 8388608 | tf_op jit(solution)/shard_map/dot_general | solution.py:24
  147.5 5.9 %fusion.10 = bf16[1,3072,256]{2,1,0:T(8,128)(2,1)} fusion(bf16[1024,256]{0,1:T(8,128)(2,1)S(1)} %get-tuple-element.18, bf16[2,1024,3072]{2,1,0:T(8,128)(2,1)} %all-gather.2.cloned.1.call-done), kind=kOutput, calls=%fused_computation.14 | convolution fusion | flops 1611399168 | bytes 8388608 | tf_op jit(solution)/shard_map/dot_general | solution.py:24
  153.4 125.1 %reduce-scatter.2.cloned.1.call-done = f32[32,3200]{1,0:T(8,128)} async-done(((f32[1024,3200]{1,0:T(8,128)}), f32[32,3200]{1,0:T(8,128)}) %reduce-scatter.2.cloned.1.call-update) | async-done | bytes 409616 | tf_op jit(solution)/shard_map/reduce_scatter | solution.py:73
  278.5 1.9 reshape.61
  280.3 6.1 %all-to-all-start.1 = ((f32[8,4,3200]{2,1,0:T(4,128)}), f32[8,4,3200]{2,1,0:T(4,128)S(1)}, u32[]{:S(2)}, u32[]{:S(2)}) async-start(f32[8,4,3200]{2,1,0:T(4,128)} %reshape.61), calls=%async_computation.2 | async-start | bytes 819200 | tf_op jit(solution)/shard_map/all_to_all | solution.py:74
  286.5 5.9 %fusion.9 = bf16[1,256,3072]{2,1,0:T(8,128)(2,1)} fusion(bf16[1024,256]{0,1:T(8,128)(2,1)S(1)} %copy-done.7, bf16[2,1024,3072]{2,1,0:T(8,128)(2,1)} %all-gather.2.cloned.1.call-done), kind=kOutput, calls=%fused_computation.13 | convolution fusion | flops 1611399168 | bytes 8388608 | tf_op jit(solution)/shard_map/dot_general | solution.py:24
  292.4 3.4 %all-to-all-done.1 = f32[8,4,3200]{2,1,0:T(4,128)S(1)} async-done(((f32[8,4,3200]{2,1,0:T(4,128)}), f32[8,4,3200]{2,1,0:T(4,128)S(1)}, u32[]{:S(2)}, u32[]{:S(2)}) %all-to-all-start.1) | async-done | bytes 409632 | tf_op jit(solution)/shard_map/all_to_all | solution.py:74
  295.8 0.1 reshape.62
  296.0 0.3 fusion.20
  296.2 0.1 slice_reduce_fusion
  296.4 0.1 reshape.63
  296.5 0.1 reduce_sum.32
  296.6 0.6 copy.19
  297.2 0.9 reduce_sum.30
  (19 shorter events, 0.2 us)
Async XLA Ops:
  7.2 101.7 %copy-start = (bf16[1,3072,256]{2,1,0:T(8,128)(2,1)S(1)}, bf16[1,3072,256]{2,1,0:T(8,128)(2,1)}, u32[]{:S(2)}) copy-start(bf16[1,3072,256]{2,1,0:T(8,128)(2,1)} %param.11) | copy-start | bytes 4718596
  7.2 101.7 %all-gather.2.cloned.1.call-start = ((), (), s32[]{:S(2)}) async-start(), calls=%async_computation.3 | async-start | bytes 12976128 | tf_op jit(solution)/shard_map/all_gather | solution.py:50
  29.3 84.3 %copy-start.2 = (bf16[1,3072,256]{2,1,0:T(8,128)(2,1)S(1)}, bf16[1,3072,256]{2,1,0:T(8,128)(2,1)}, u32[]{:S(2)}) copy-start(bf16[1,3072,256]{2,1,0:T(8,128)(2,1)} %param.12) | copy-start | bytes 4718596
  29.3 249.2 %reduce-scatter.2.cloned.1.call-start = ((), (), s32[]{:S(2)}) async-start(), calls=%async_computation.4 | async-start | bytes 13516800 | tf_op jit(solution)/shard_map/reduce_scatter | solution.py:73
  108.8 6.4 %copy-start.5 = (bf16[2,1024,3072]{2,1,0:T(8,128)(2,1)S(1)}, bf16[2,1024,3072]{2,1,0:T(8,128)(2,1)}, u32[]{:S(2)}) copy-start(bf16[2,1024,3072]{2,1,0:T(8,128)(2,1)} %all-gather.2.cloned.1.call-done) | copy-start | bytes 37748740
  115.2 1.9 copy-start.6
  120.5 3.0 copy-start.3
  140.4 1.0 copy-start.4
  147.5 139.0 %copy-start.7 = (bf16[1024,256]{0,1:T(8,128)(2,1)S(1)}, bf16[1024,256]{0,1:T(8,128)(2,1)}, u32[]{:S(2)}) copy-start(bf16[1024,256]{0,1:T(8,128)(2,1)} %get-tuple-element.16) | copy-start | bytes 1572868
  280.3 15.5 %all-to-all-start.1 = ((f32[8,4,3200]{2,1,0:T(4,128)}), f32[8,4,3200]{2,1,0:T(4,128)S(1)}, u32[]{:S(2)}, u32[]{:S(2)}) async-start(f32[8,4,3200]{2,1,0:T(4,128)} %reshape.61), calls=%async_computation.2 | async-start | bytes 819200 | tf_op jit(solution)/shard_map/all_to_all | solution.py:74
  286.5 11.6 %copy-start.1 = (bf16[1,3072,256]{2,1,0:T(8,128)(2,1)S(1)}, bf16[1,3072,256]{2,1,0:T(8,128)(2,1)}, u32[]{:S(2)}) copy-start(bf16[1,3072,256]{2,1,0:T(8,128)(2,1)} %param.11) | copy-start | bytes 4718596
Sparse Core Ops, SparseCore 0:
  29.4 79.3 all-gather.1
  140.5 137.8 reduce-scatter.1
where the time goes:
time: 305 us
  waiting for transfers between devices  208 us (68%)
  matrix products  38 us (12%)
  blocking collectives  16 us (5%)
  between operations  14.2 us (5%)
  other arithmetic  12.6 us (4%)
  local copies, waits for them, and re-layouts  9.78 us (3%)
  starting transfers between devices  6.22 us (2%)
    reduce_scatter x1, waiting for transfers between devices, local(): lax.psum_scatter(part, 'section', scatter_dimension=0, tiled=True)  125 us
    all_gather x1, waiting for transfers between devices, local(): every = lax.all_gather(mine, 'section', axis=1, tiled=True)  79.5 us
    dot_general x5, matrix products, contract_first(): lax.dot_general(left, right, (((0,), (0,)), ((), ())), preferred_element_...  18.4 us
    all_to_all x1, blocking collectives, local(): lax.all_to_all(send, 'expert', split_axis=0, concat_axis=0, tiled=True)  16 us
    dot_general x3, matrix products, contract_last(): lax.dot_general(left, right, (((1,), (1,)), ((), ())), preferred_element_...  12.7 us
    concatenate x1, other arithmetic, local(): part = jnp.concatenate([input_part, gate_part], axis=1)  10.3 us
    all_to_all x1, starting transfers between devices, local(): lax.all_to_all(part_mine.reshape(experts, capacity, features + 128), 'exp...  6.14 us
  transfers between devices with their start and end apart: 3, of which 3 were waited for; matrix products, arithmetic and copies ran while one was open for 6% of the time, Pallas kernels for 0%

commit v1 on v0

--- a/solution.py
+++ b/solution.py
@@ -2,6 +2,13 @@
 import jax.numpy as jnp
 from jax import lax
 from jax.sharding import PartitionSpec as P
+
+
+def all_by_exchange(shard, axis, d):
+    size = lax.axis_size(axis)
+    shards = jnp.stack([shard for _ in range(size)])
+    shards = lax.all_to_all(shards, axis, split_axis=0, concat_axis=0)
+    return jnp.concatenate(shards, axis=d)
 
 
 def slot_matrix(route_ids, experts, capacity):
@@ -47,7 +54,7 @@
     mine = jnp.stack([recv[:, :capacity], recv[:, capacity:]]).reshape(
         2, experts * capacity, features
     )
-    every = lax.all_gather(mine, "section", axis=1, tiled=True)
+    every = all_by_exchange(mine, "section", 1)
     rows_x, rows_u = (every[0], every[1])
     gate_slab = w_gate[0]
     up_slab = w_up[0]

time: 305 us -> 510 us (1.67)
  blocking collectives: 16 us -> 301 us
  waiting for transfers between devices: 208 us -> 123 us
  local copies, waits for them, and re-layouts: 9.78 us -> 18.4 us
    all_to_all x0 -> x1, blocking collectives: none -> 285 us  [all_by_exchange(): shards = lax.all_to_all(shards, axis, split_axis=0, concat_axis=0)]
    all_gather x1 -> x0, waiting for transfers between devices: 79.5 us -> none  [local(): every = lax.all_gather(mine, 'section', axis=1, tiled=True)]
    another operation x0 -> x1, local copies, waits for them, and re-layouts: none -> 6.15 us  [all_by_exchange(): shards = jnp.stack([shard for _ in range(size)])]
  transfers between devices with their start and end apart: 3 -> 2, of which waited for: 3 -> 2; matrix products, arithmetic and copies ran while one was open for 6% -> 3% of each run, Pallas kernels for 0% -> 0%
where the time goes in v1:
time: 510 us
  blocking collectives  301 us (59%)
  waiting for transfers between devices  123 us (24%)
  matrix products  35 us (7%)
  local copies, waits for them, and re-layouts  18.4 us (4%)
  between operations  14.3 us (3%)
  other arithmetic  11.9 us (2%)
  starting transfers between devices  6.19 us (1%)
    all_to_all x1, blocking collectives, all_by_exchange(): shards = lax.all_to_all(shards, axis, split_axis=0, concat_axis=0)  285 us
    reduce_scatter x1, waiting for transfers between devices, local(): lax.psum_scatter(part, 'section', scatter_dimension=0, tiled=True)  120 us
    dot_general x5, matrix products, contract_first(): lax.dot_general(left, right, (((0,), (0,)), ((), ())), preferred_element_...  18.4 us
    all_to_all x1, blocking collectives, local(): lax.all_to_all(send, 'expert', split_axis=0, concat_axis=0, tiled=True)  16 us
    dot_general x3, matrix products, contract_last(): lax.dot_general(left, right, (((1,), (1,)), ((), ())), preferred_element_...  12.6 us
    concatenate x1, other arithmetic, local(): part = jnp.concatenate([input_part, gate_part], axis=1)  10.3 us
  transfers between devices with their start and end apart: 2, of which 2 were waited for; matrix products, arithmetic and copies ran while one was open for 3% of the time, Pallas kernels for 0%

profile of v1, /device:TPU:2, one launch (start us, length us, event | category | flops | bytes accessed | tf_op | source)
XLA Modules:
  0.0 509.8 jit_solution(6853871788540877860)
XLA Ops:
  7.2 0.0 copy-start
  7.2 0.0 reduce-scatter.2.cloned.1.call-start
  7.2 0.9 copy.17
  8.1 0.1 reshape.73
  8.2 0.8 copy.16
  8.9 0.1 reshape.65
  9.0 0.1 fusion.15
  9.1 0.2 select_reduce_fusion
  9.3 0.9 broadcast_in_dim.19
  10.2 0.3 convolution_convert_fusion.4
  10.5 0.1 reshape.67
  10.6 0.9 broadcast_in_dim.20
  11.5 0.1 convert_element_type.63
  11.6 0.3 convolution_convert_fusion.3
  11.9 0.1 reshape.68
  12.0 0.2 pad_maximum_fusion.1
  12.2 16.0 %all_to_all.15 = bf16[8,8,3072]{2,1,0:T(8,128)(2,1)S(1)} all-to-all(bf16[8,8,3072]{2,1,0:T(8,128)(2,1)S(1)} %pad_maximum_fusion.1), channel_id=1, replica_groups=mesh['section'=32,'expert'=8] {'expert'}, dimensions={0} | all-to-all | bytes 786432 | tf_op jit(solution)/shard_map/all_to_all | solution.py:53
  28.3 0.1 fusion.20
  28.5 6.2 %stack.15 = bf16[32,2,32,3072]{3,2,1,0:T(8,128)(2,1)} broadcast(bf16[2,32,3072]{2,1,0:T(8,128)(2,1)S(1)} %maximum_bitcast_fusion), dimensions={1,2,3} | broadcast | bytes 12976128 | tf_op jit(solution)/shard_map/stack | solution.py:9
  34.7 284.6 %all_to_all.16 = bf16[32,2,32,3072]{3,2,1,0:T(8,128)(2,1)S(1)} all-to-all(bf16[32,2,32,3072]{3,2,1,0:T(8,128)(2,1)} %stack.15), channel_id=1, replica_groups=mesh['section'=32,'expert'=8] {'section'}, dimensions={0} | all-to-all | bytes 25165824 | tf_op jit(solution)/shard_map/all_to_all | solution.py:10
  319.3 2.6 fusion.19
  322.0 1.9 fusion.5
  323.9 0.8 copy-done.3
  324.7 1.9 fusion.8
  326.6 0.6 copy-done.2
  327.1 0.1 copy-done.7
  327.2 3.2 convert_multiply_fusion
  330.4 0.1 slice_add_fusion
  330.4 0.2 copy.18
  330.6 3.0 fusion.3
  333.7 6.4 %convolution_add_fusion = f32[1024,3072]{1,0:T(8,128)} fusion(f32[1024,3072]{1,0:T(8,128)S(1)} %fusion.3, bf16[1024,256]{0,1:T(8,128)(2,1)S(1)} %get-tuple-element.20, bf16[1,3072,256]{2,1,0:T(8,128)(2,1)S(1)} %copy-done.5), kind=kOutput, calls=%fused_computation.1 | convolution fusion | flops 1613758464 | bytes 27262976 | tf_op jit(solution)/shard_map/dot_general | solution.py:25
  340.1 10.3 %pad_maximum_fusion = f32[1024,3200]{1,0:T(8,128)} fusion(f32[1024,128]{1,0:T(8,128)S(1)} %copy.18, f32[1024,3072]{1,0:T(8,128)} %convolution_add_fusion), kind=kLoop, calls=%fused_computation | loop fusion | flops 3276800 | bytes 26214400 | tf_op jit(solution)/shard_map/concatenate | solution.py:79
  350.4 0.0 reduce-scatter.2.cloned.1.call-update
  350.4 1.0 copy-done.6
  351.4 6.1 %fusion = bf16[1,3072,256]{2,1,0:T(8,128)(2,1)} fusion(bf16[1024,3072]{1,0:T(8,128)(2,1)} %bitcast.44, bf16[1024,256]{0,1:T(8,128)(2,1)S(1)} %copy-done.6), kind=kOutput, calls=%fused_computation.5 | convolution fusion | flops 1611399168 | bytes 8388608 | tf_op jit(solution)/shard_map/dot_general | solution.py:31
  357.5 5.9 %fusion.1 = bf16[1,3072,256]{2,1,0:T(8,128)(2,1)} fusion(bf16[1024,3072]{1,0:T(8,128)(2,1)} %bitcast.45, bf16[1024,256]{0,1:T(8,128)(2,1)S(1)} %get-tuple-element.20), kind=kOutput, calls=%fused_computation.6 | convolution fusion | flops 1611399168 | bytes 8388608 | tf_op jit(solution)/shard_map/dot_general | solution.py:31
  363.4 120.0 %reduce-scatter.2.cloned.1.call-done = f32[32,3200]{1,0:T(8,128)} async-done(((f32[1024,3200]{1,0:T(8,128)}), f32[32,3200]{1,0:T(8,128)}) %reduce-scatter.2.cloned.1.call-update) | async-done | bytes 409616 | tf_op jit(solution)/shard_map/reduce_scatter | solution.py:80
  483.4 1.9 reshape.70
  485.2 6.1 %all-to-all-start.2 = ((f32[8,4,3200]{2,1,0:T(4,128)}), f32[8,4,3200]{2,1,0:T(4,128)S(1)}, u32[]{:S(2)}, u32[]{:S(2)}) async-start(f32[8,4,3200]{2,1,0:T(4,128)} %reshape.70), calls=%async_computation.3 | async-start | bytes 819200 | tf_op jit(solution)/shard_map/all_to_all | solution.py:81
  491.4 5.8 %fusion.2 = bf16[1,256,3072]{2,1,0:T(8,128)(2,1)} fusion(bf16[1024,256]{0,1:T(8,128)(2,1)S(1)} %copy-done.8, bf16[1024,3072]{1,0:T(8,128)(2,1)} %bitcast.41), kind=kOutput, calls=%fused_computation.7 | convolution fusion | flops 1611399168 | bytes 8388608 | tf_op jit(solution)/shard_map/dot_general | solution.py:31
  497.2 3.5 all-to-all-done.2
  500.7 0.1 reshape.71
  500.9 0.3 fusion.14
  501.1 0.1 slice_reduce_fusion
  501.3 0.1 reshape.72
  501.4 0.1 reduce_sum.32
  501.5 0.6 copy.19
  502.1 0.9 reduce_sum.30
  (21 shorter events, 0.3 us)
Async XLA Ops:
  7.2 314.8 %copy-start = (bf16[1,3072,256]{2,1,0:T(8,128)(2,1)S(1)}, bf16[1,3072,256]{2,1,0:T(8,128)(2,1)}, u32[]{:S(2)}) copy-start(bf16[1,3072,256]{2,1,0:T(8,128)(2,1)} %param.11) | copy-start | bytes 4718596
  7.2 476.2 %reduce-scatter.2.cloned.1.call-start = ((), (), s32[]{:S(2)}) async-start(), calls=%async_computation.4 | async-start | bytes 13516800 | tf_op jit(solution)/shard_map/reduce_scatter | solution.py:80
  322.0 2.7 copy-start.3
  322.0 5.1 %copy-start.2 = (bf16[1,32,32,3072]{3,2,0,1:T(8,128)(2,1)}, bf16[1,32,32,3072]{3,2,0,1:T(8,128)(2,1)S(1)}, u32[]{:S(2)}) copy-start(bf16[1,32,32,3072]{3,2,0,1:T(8,128)(2,1)S(1)} %get-tuple-element.18) | copy-start | bytes 18874372
  322.0 2.7 copy-start.4
  324.7 2.5 copy-start.7
  330.6 3.0 copy-start.5
  350.4 1.0 copy-start.6
  357.5 133.9 %copy-start.8 = (bf16[1024,256]{0,1:T(8,128)(2,1)S(1)}, bf16[1024,256]{0,1:T(8,128)(2,1)}, u32[]{:S(2)}) copy-start(bf16[1024,256]{0,1:T(8,128)(2,1)} %get-tuple-element.16) | copy-start | bytes 1572868
  485.2 15.5 %all-to-all-start.2 = ((f32[8,4,3200]{2,1,0:T(4,128)}), f32[8,4,3200]{2,1,0:T(4,128)S(1)}, u32[]{:S(2)}, u32[]{:S(2)}) async-start(f32[8,4,3200]{2,1,0:T(4,128)} %reshape.70), calls=%async_computation.3 | async-start | bytes 819200 | tf_op jit(solution)/shard_map/all_to_all | solution.py:81
  491.4 11.6 %copy-start.1 = (bf16[1,3072,256]{2,1,0:T(8,128)(2,1)S(1)}, bf16[1,3072,256]{2,1,0:T(8,128)(2,1)}, u32[]{:S(2)}) copy-start(bf16[1,3072,256]{2,1,0:T(8,128)(2,1)} %param.11) | copy-start | bytes 4718596
Sparse Core Ops, SparseCore 0:
  350.5 132.8 reduce-scatter.1
